TPU v7x, 256 devices: a whole 4x4x8 slice. The times are simulated.
256 devices in a mesh: dp: 4 (over y), blocks: 64 (over x, z, core).
Axes of the slice: x: 4, y: 4, z: 8, core: 2. Of those that a mesh axis runs over, the one named last changes fastest.
Arguments:
- tokens: bfloat16 [16384, 8192], P('blocks', 'dp'), may hold values from -6 to 6
- dec_bias: float32 [8192], P('dp'), may hold values from -3 to 3
- routes: int32 [16384, 2], P('blocks'), may hold values from 0 to 63, all different within a row; in each aligned block of 256 rows (0 to 255, 256 to 511, ...) at most 16 rows name the same one
- latent_picks: int32 [16384, 2, 16], P('blocks'), may hold values from 0 to 1023
- enc_weight: bfloat16 [64, 8192, 1024], P('blocks', 'dp'), may hold values from -0.0625 to 0.0625
- dec_weight: bfloat16 [64, 1024, 8192], P('blocks', None, 'dp'), may hold values from -1 to 1
- enc_bias: float32 [64, 1024], P('blocks'), may hold values from -3 to 3
Outputs:
- reconstruction: bfloat16 [16384, 8192], P('blocks', 'dp')
Inputs may be any that keep to these rules, and one draw needn't show every extreme that they name: `routes`: each row names 2 different blocks; among the rows of one index of blocks no block is named by more than 16 rows, and some block by exactly 16. `latent_picks`: indices within a block; a row may name an index more than once.
All inputs are finite; a program needn't handle non-finite values.
Results may differ from a plain program's by a relative error of at most 0.0059.
Values may be sent and summed in bfloat16 or wider, within the bound.
A program may use at most 64 MiB of HBM per device.

v0:
```python
import jax
import jax.numpy as jnp
from jax import lax
from jax.sharding import PartitionSpec as P


def on_device(tokens, dec_bias, routes, latent_picks, enc_weight, dec_weight, enc_bias):
    tok_rows, quarter = tokens.shape
    top_blocks = routes.shape[1]
    pick_count = latent_picks.shape[2]
    latents = enc_weight.shape[2]
    blk_count = lax.axis_size("blocks")
    capacity = max(2, 2 * tok_rows * top_blocks // blk_count)
    slot_count = blk_count * capacity
    pair_count = tok_rows * top_blocks
    centered = (tokens.astype(jnp.float32) - dec_bias).astype(jnp.bfloat16)
    owners = routes.reshape(pair_count)
    onehot = (owners[:, None] == jnp.arange(blk_count, dtype=jnp.int32)[None, :]).astype(jnp.int32)
    slot_rank = jnp.sum(jnp.cumsum(onehot, axis=0) * onehot, axis=1) - 1
    target = owners * capacity + slot_rank
    placing = jnp.arange(slot_count, dtype=jnp.int32)[:, None] == target[None, :]
    place_half = placing.astype(jnp.bfloat16)
    paired = jnp.repeat(centered, top_blocks, axis=0)
    outgoing = jnp.dot(place_half, paired, preferred_element_type=jnp.float32).astype(jnp.bfloat16)
    outgoing = outgoing.reshape(blk_count, capacity, quarter)
    sent_picks = jnp.dot(
        placing.astype(jnp.float32),
        latent_picks.reshape(pair_count, pick_count).astype(jnp.float32),
        precision=lax.Precision.HIGHEST,
    ).astype(jnp.int32)
    sent_picks = sent_picks.reshape(blk_count, capacity, pick_count)
    enc_local = enc_weight[0]
    dec_local = dec_weight[0]
    bias_local = enc_bias[0]
    lat_ids = jnp.arange(latents, dtype=jnp.int32)
    arrived = lax.all_to_all(outgoing, "blocks", split_axis=0, concat_axis=0, tiled=True)
    chosen = lax.all_to_all(sent_picks, "blocks", split_axis=0, concat_axis=0, tiled=True)
    item_count = arrived.shape[1]
    flat_rows = arrived.reshape(blk_count * item_count, quarter)
    chosen_ids = chosen.reshape(blk_count * item_count, pick_count)
    partial_value = jnp.dot(flat_rows, enc_local, preferred_element_type=jnp.float32)
    summed = lax.psum(partial_value, "dp") + bias_local[None, :]
    keep_mask = jnp.any(chosen_ids[:, :, None] == lat_ids[None, None, :], axis=1)
    active = jnp.where(keep_mask, jnp.maximum(summed, 0.0), 0.0).astype(jnp.bfloat16)
    partial_out = jnp.dot(active, dec_local, preferred_element_type=jnp.float32).astype(
        jnp.bfloat16
    )
    partial_out = partial_out.reshape(blk_count, item_count, quarter)
    returned = lax.all_to_all(partial_out, "blocks", split_axis=0, concat_axis=0, tiled=True)
    back_rows = returned.reshape(slot_count, quarter)
    per_pair = jnp.einsum("sp,sd->pd", place_half, back_rows, preferred_element_type=jnp.float32)
    summed_out = per_pair.reshape(tok_rows, top_blocks, quarter).sum(axis=1) + dec_bias
    return summed_out.astype(jnp.bfloat16)


def solution(mesh):
    in_specs = (
        P("blocks", "dp"),
        P("dp"),
        P("blocks", None),
        P("blocks", None, None),
        P("blocks", "dp", None),
        P("blocks", None, "dp"),
        P("blocks", None),
    )
    out_specs = P("blocks", "dp")
    return jax.shard_map(
        on_device, mesh=mesh, in_specs=in_specs, out_specs=out_specs, check_vma=False
    )
```

profile of v0, /device:TPU:1, one launch (start us, length us, event | category | flops | bytes accessed | tf_op | source)
XLA Modules:
  0.0 357.7 jit_solution(9807614320305272181)
XLA Ops:
  6.5 0.8 copy.23
  7.7 1.2 reduce-window.6
  8.9 0.2 slice_reduce_fusion
  9.3 1.5 subtract_convert_fusion
  10.8 1.3 broadcast_in_dim.3
  12.1 2.2 reshape.80
  14.3 3.9 %convolution_convert_fusion = bf16[1024,2048]{1,0:T(8,128)(2,1)S(1)} fusion(bf16[512,2048]{1,0:T(8,128)(2,1)} %reshape.80, s32[512]{0:T(512)S(1)} %add_add_fusion), kind=kOutput, calls=%fused_computation.7 | convolution fusion | flops 2150105088 | bytes 6293504 | tf_op jit(solution)/shard_map/dot_general | solution.py:24
  18.2 109.2 %all_to_all.15 = bf16[64,16,2048]{2,1,0:T(8,128)(2,1)S(1)} all-to-all(bf16[64,16,2048]{2,1,0:T(8,128)(2,1)S(1)} %bitcast.43), channel_id=1, replica_groups=mesh['dp'=4,'blocks'=64] {'blocks'}, dimensions={0} | all-to-all | bytes 8388608 | tf_op jit(solution)/shard_map/all_to_all | solution.py:36
  127.5 6.0 %fusion.3 = f32[1024,1024]{1,0:T(8,128)} fusion(bf16[1024,2048]{1,0:T(8,128)(2,1)S(1)} %bitcast.44, bf16[1,2048,1024]{2,1,0:T(8,128)(2,1)S(1)} %copy-done.2), kind=kOutput, calls=%fused_computation.4 | convolution fusion | flops 4294967296 | bytes 12582912 | tf_op jit(solution)/shard_map/dot_general | solution.py:41
  133.6 0.7 copy-done.1
  134.4 1.0 fusion.16
  135.7 0.3 copy.40
  136.2 15.4 %all_to_all.16 = s32[64,1,256]{2,1,0:T(1,128)S(1)} all-to-all(s32[64,1,256]{2,1,0:T(1,128)S(1)} %reshape.87), channel_id=1, replica_groups=mesh['dp'=4,'blocks'=64] {'blocks'}, dimensions={0} | all-to-all | bytes 131072 | tf_op jit(solution)/shard_map/all_to_all | solution.py:37
  151.7 0.5 broadcast.47
  152.2 0.8 reduce.2
  153.4 13.1 %fusion = pred[1024,1024]{1,0:T(8,128)(4,1)S(1)} fusion(s32[1024,16]{1,0:T(8,128)S(1)} %bitcast.45), kind=kLoop, calls=%fused_computation.1 | loop fusion | flops 32505856 | bytes 1114112 | tf_op jit(solution)/shard_map/reduce_or | solution.py:43
  166.5 61.8 %all-reduce.2.cloned.1.call-done = f32[1024,1024]{1,0:T(8,128)} async-done(((f32[1024,1024]{1,0:T(8,128)}), f32[1024,1024]{1,0:T(8,128)}) %all-reduce.2.cloned.1.call-update) | async-done | bytes 4194320 | tf_op jit(solution)/shard_map/psum | solution.py:42
  228.3 10.0 %fusion.5 = bf16[1024,2048]{1,0:T(8,128)(2,1)} fusion(bf16[1,1024,2048]{2,1,0:T(8,128)(2,1)} %param.12, pred[1024,1024]{1,0:T(8,128)(4,1)S(1)} %fusion, f32[1024,1024]{1,0:T(8,128)} %all-reduce.2.cloned.1.call-done, f32[1024]{0:T(1024)S(1)} %bitcast.49), kind=kOutput, calls=%fused_computation.8 | convolution fusion | flops 4301258752 | bytes 13635584 | tf_op jit(solution)/shard_map/dot_general | solution.py:45
  238.3 10.8 %all-to-all-start.2 = ((bf16[64,16,2048]{2,1,0:T(8,128)(2,1)}), bf16[64,16,2048]{2,1,0:T(8,128)(2,1)}, u32[]{:S(2)}, u32[]{:S(2)}) async-start(bf16[64,16,2048]{2,1,0:T(8,128)(2,1)} %bitcast.42), calls=%async_computation.2 | async-start | bytes 8388608 | tf_op jit(solution)/shard_map/all_to_all | solution.py:49
  249.1 0.4 iota_compare_fusion.4
  249.5 1.0 eq.76
  250.5 94.5 %all-to-all-done.2 = bf16[64,16,2048]{2,1,0:T(8,128)(2,1)} async-done(((bf16[64,16,2048]{2,1,0:T(8,128)(2,1)}), bf16[64,16,2048]{2,1,0:T(8,128)(2,1)}, u32[]{:S(2)}, u32[]{:S(2)}) %all-to-all-start.2) | async-done | bytes 4194336 | tf_op jit(solution)/shard_map/all_to_all | solution.py:49
  345.0 4.7 %fusion.13 = f32[256,2048]{1,0:T(8,128)S(1)} fusion(bf16[1024,2048,1]{1,0,2:T(8,128)(2,1)} %bitcast.10, pred[256,2,1024]{2,1,0:T(4,128)(4,1)S(1)} %eq.76), kind=kOutput, calls=%fused_computation.18 | convolution fusion | flops 2148007936 | bytes 6815744 | tf_op jit(solution)/shard_map/sp,sd->pd/dot_general | solution.py:51
  349.7 1.2 add_convert_fusion
  (22 shorter events, 1.5 us)
Async XLA Ops:
  6.5 221.8 %all-reduce.2.cloned.1.call-start = ((), (), s32[]{:S(2)}) async-start(), calls=%async_computation.3 | async-start | bytes 8388608 | tf_op jit(solution)/shard_map/psum | solution.py:42
  18.2 109.3 %copy-start.2 = (bf16[1,2048,1024]{2,1,0:T(8,128)(2,1)S(1)}, bf16[1,2048,1024]{2,1,0:T(8,128)(2,1)}, u32[]{:S(2)}) copy-start(bf16[1,2048,1024]{2,1,0:T(8,128)(2,1)} %param.11) | copy-start | bytes 12582916
  133.5 0.8 copy-start.1
  134.3 94.0 %copy-start.3 = (f32[1,1024]{1,0:T(1,128)S(1)}, f32[1,1024]{1,0:T(1,128)}, u32[]{:S(2)}) copy-start(f32[1,1024]{1,0:T(1,128)} %param.13) | copy-start | bytes 12292
  238.3 106.7 %all-to-all-start.2 = ((bf16[64,16,2048]{2,1,0:T(8,128)(2,1)}), bf16[64,16,2048]{2,1,0:T(8,128)(2,1)}, u32[]{:S(2)}, u32[]{:S(2)}) async-start(bf16[64,16,2048]{2,1,0:T(8,128)(2,1)} %bitcast.42), calls=%async_computation.2 | async-start | bytes 8388608 | tf_op jit(solution)/shard_map/all_to_all | solution.py:49
  345.0 4.7 %copy-start = (f32[2048]{0:T(1024)S(1)}, f32[2048]{0:T(1024)}, u32[]{:S(2)}) copy-start(f32[2048]{0:T(1024)} %param.8) | copy-start | bytes 24580
Sparse Core Ops, SparseCore 0:
  133.7 94.5 all-reduce.1
where the time goes:
time: 358 us
  waiting for transfers between devices  156 us (44%)
  blocking collectives  125 us (35%)
  matrix products  25.6 us (7%)
  other arithmetic  18.3 us (5%)
  between operations  13.6 us (4%)
  starting transfers between devices  10.8 us (3%)
  local copies, waits for them, and re-layouts  8.35 us (2%)
    all_to_all x1, blocking collectives, on_device(): lax.all_to_all(outgoing, 'blocks', split_axis=0, concat_axis=0, tiled=True)  109 us
    all_to_all x1, waiting for transfers between devices, on_device(): lax.all_to_all(partial_out, 'blocks', split_axis=0, concat_axis=0, tiled=...  94.5 us
    psum x1, waiting for transfers between devices, on_device(): summed = lax.psum(partial_value, 'dp') + bias_local[None, :]  61.8 us
    all_to_all x1, blocking collectives, on_device(): lax.all_to_all(sent_picks, 'blocks', split_axis=0, concat_axis=0, tiled=T...  15.4 us
    reduce_or x1, other arithmetic, on_device(): jnp.any(chosen_ids[:, :, None] == lat_ids[None, None, :], axis=1)  13.1 us
    all_to_all x1, starting transfers between devices, on_device(): lax.all_to_all(partial_out, 'blocks', split_axis=0, concat_axis=0, tiled=...  10.8 us
    dot_general x1, matrix products, on_device(): jnp.dot(active, dec_local, preferred_element_type=jnp.float32)  9.97 us
  transfers between devices with their start and end apart: 2, of which 2 were waited for; matrix products, arithmetic and copies ran while one was open for 5% of the time, Pallas kernels for 0%

commit v1 on v0

--- a/solution.py
+++ b/solution.py
@@ -2,6 +2,10 @@
 import jax.numpy as jnp
 from jax import lax
 from jax.sharding import PartitionSpec as P
+
+
+def _follow_runs(row_data, along_axis):
+    return jax.lax.all_gather(row_data, along_axis).sum(axis=0)
 
 
 def on_device(tokens, dec_bias, routes, latent_picks, enc_weight, dec_weight, enc_bias):
@@ -39,7 +43,7 @@
     flat_rows = arrived.reshape(blk_count * item_count, quarter)
     chosen_ids = chosen.reshape(blk_count * item_count, pick_count)
     partial_value = jnp.dot(flat_rows, enc_local, preferred_element_type=jnp.float32)
-    summed = lax.psum(partial_value, "dp") + bias_local[None, :]
+    summed = _follow_runs(partial_value, along_axis="dp") + bias_local[None, :]
     keep_mask = jnp.any(chosen_ids[:, :, None] == lat_ids[None, None, :], axis=1)
     active = jnp.where(keep_mask, jnp.maximum(summed, 0.0), 0.0).astype(jnp.bfloat16)
     partial_out = jnp.dot(active, dec_local, preferred_element_type=jnp.float32).astype(

time: 358 us -> 427 us (1.19)
  waiting for transfers between devices: 156 us -> 215 us
  other arithmetic: 18.3 us -> 28.6 us
    all_gather x0 -> x1, waiting for transfers between devices: none -> 121 us  [_follow_runs(): return jax.lax.all_gather(row_data, along_axis).sum(axis=0)]
    psum x1 -> x0, waiting for transfers between devices: 61.8 us -> none  [on_device(): summed = lax.psum(partial_value, 'dp') + bias_local[None, :]]
    reduce_sum x0 -> x1, other arithmetic: none -> 10.3 us  [_follow_runs(): return jax.lax.all_gather(row_data, along_axis).sum(axis=0)]
  transfers between devices with their start and end apart: 2 -> 2, of which waited for: 2 -> 2; matrix products, arithmetic and copies ran while one was open for 5% -> 4% of each run, Pallas kernels for 0% -> 0%
where the time goes in v1:
time: 427 us
  waiting for transfers between devices  215 us (50%)
  blocking collectives  125 us (29%)
  other arithmetic  28.6 us (7%)
  matrix products  25.5 us (6%)
  between operations  13.6 us (3%)
  starting transfers between devices  10.8 us (3%)
  local copies, waits for them, and re-layouts  8.35 us (2%)
    all_gather x1, waiting for transfers between devices, _follow_runs(): return jax.lax.all_gather(row_data, along_axis).sum(axis=0)  121 us
    all_to_all x1, blocking collectives, on_device(): lax.all_to_all(outgoing, 'blocks', split_axis=0, concat_axis=0, tiled=True)  109 us
    all_to_all x1, waiting for transfers between devices, on_device(): lax.all_to_all(partial_out, 'blocks', split_axis=0, concat_axis=0, tiled=...  94.5 us
    all_to_all x1, blocking collectives, on_device(): lax.all_to_all(sent_picks, 'blocks', split_axis=0, concat_axis=0, tiled=T...  15.4 us
    reduce_or x1, other arithmetic, on_device(): jnp.any(chosen_ids[:, :, None] == lat_ids[None, None, :], axis=1)  13.1 us
    all_to_all x1, starting transfers between devices, on_device(): lax.all_to_all(partial_out, 'blocks', split_axis=0, concat_axis=0, tiled=...  10.8 us
    reduce_sum x1, other arithmetic, _follow_runs(): return jax.lax.all_gather(row_data, along_axis).sum(axis=0)  10.3 us
    dot_general x1, matrix products, on_device(): jnp.dot(active, dec_local, preferred_element_type=jnp.float32)  9.9 us
  transfers between devices with their start and end apart: 2, of which 2 were waited for; matrix products, arithmetic and copies ran while one was open for 4% of the time, Pallas kernels for 0%

profile of v1, /device:TPU:1, one launch (start us, length us, event | category | flops | bytes accessed | tf_op | source)
XLA Modules:
  0.0 426.6 jit_solution(12763269797102371363)
XLA Ops:
  6.5 0.8 copy.23
  7.7 1.2 reduce-window.6
  9.3 1.5 subtract_convert_fusion
  10.8 1.3 broadcast_in_dim.3
  12.1 2.2 reshape.80
  14.3 3.9 convolution_convert_fusion
  18.2 109.2 %all_to_all.15 = bf16[64,16,2048]{2,1,0:T(8,128)(2,1)S(1)} all-to-all(bf16[64,16,2048]{2,1,0:T(8,128)(2,1)S(1)} %bitcast.45), channel_id=1, replica_groups=mesh['dp'=4,'blocks'=64] {'blocks'}, dimensions={0} | all-to-all | bytes 8388608 | tf_op jit(solution)/shard_map/all_to_all | solution.py:40
  127.5 6.0 %fusion.3 = f32[1024,1024]{1,0:T(8,128)} fusion(bf16[1024,2048]{1,0:T(8,128)(2,1)S(1)} %bitcast.46, bf16[1,2048,1024]{2,1,0:T(8,128)(2,1)S(1)} %copy-done.2), kind=kOutput, calls=%fused_computation.4 | convolution fusion | flops 4294967296 | bytes 12582912 | tf_op jit(solution)/shard_map/dot_general | solution.py:45
  133.5 0.7 copy-done.1
  134.4 1.0 fusion.16
  135.7 0.3 copy.40
  136.2 15.4 %all_to_all.16 = s32[64,1,256]{2,1,0:T(1,128)S(1)} all-to-all(s32[64,1,256]{2,1,0:T(1,128)S(1)} %reshape.88), channel_id=1, replica_groups=mesh['dp'=4,'blocks'=64] {'blocks'}, dimensions={0} | all-to-all | bytes 131072 | tf_op jit(solution)/shard_map/all_to_all | solution.py:41
  151.6 0.5 broadcast.47
  152.1 0.8 reduce.2
  153.4 13.1 %fusion = pred[1024,1024]{1,0:T(8,128)(4,1)S(1)} fusion(s32[1024,16]{1,0:T(8,128)S(1)} %bitcast.47), kind=kLoop, calls=%fused_computation.1 | loop fusion | flops 32505856 | bytes 1114112 | tf_op jit(solution)/shard_map/reduce_or | solution.py:47
  166.5 120.5 %all-gather.3.cloned.1.call-done = f32[4096,1024]{1,0:T(8,128)} async-done(((f32[1024,1024]{1,0:T(8,128)}), f32[4096,1024]{1,0:T(8,128)}) %all-gather.3.cloned.1.call-update) | async-done | bytes 16777232 | tf_op jit(solution)/shard_map/all_gather | solution.py:8
  287.0 10.3 %reduce_sum.28 = f32[1024,1024]{1,0:T(8,128)} reduce(f32[4,1024,1024]{2,1,0:T(8,128)} %bitcast.43, f32[]{:T(128)} %constant.15.clone.1), dimensions={0}, to_apply=%region_4.5 | reduce | flops 3145728 | bytes 20971524 | tf_op jit(solution)/shard_map/reduce_sum | solution.py:8
  297.3 9.9 %fusion.5 = bf16[1024,2048]{1,0:T(8,128)(2,1)} fusion(bf16[1,1024,2048]{2,1,0:T(8,128)(2,1)} %param.12, pred[1024,1024]{1,0:T(8,128)(4,1)S(1)} %fusion, f32[1024,1024]{1,0:T(8,128)} %reduce_sum.28, f32[1024]{0:T(1024)S(1)} %bitcast.51), kind=kOutput, calls=%fused_computation.8 | convolution fusion | flops 4301258752 | bytes 13635584 | tf_op jit(solution)/shard_map/dot_general | solution.py:49
  307.2 10.8 %all-to-all-start.2 = ((bf16[64,16,2048]{2,1,0:T(8,128)(2,1)}), bf16[64,16,2048]{2,1,0:T(8,128)(2,1)}, u32[]{:S(2)}, u32[]{:S(2)}) async-start(bf16[64,16,2048]{2,1,0:T(8,128)(2,1)} %bitcast.44), calls=%async_computation.2 | async-start | bytes 8388608 | tf_op jit(solution)/shard_map/all_to_all | solution.py:53
  318.0 0.4 iota_compare_fusion.4
  318.4 1.0 eq.76
  319.4 94.5 %all-to-all-done.2 = bf16[64,16,2048]{2,1,0:T(8,128)(2,1)} async-done(((bf16[64,16,2048]{2,1,0:T(8,128)(2,1)}), bf16[64,16,2048]{2,1,0:T(8,128)(2,1)}, u32[]{:S(2)}, u32[]{:S(2)}) %all-to-all-start.2) | async-done | bytes 4194336 | tf_op jit(solution)/shard_map/all_to_all | solution.py:53
  413.9 4.7 %fusion.13 = f32[256,2048]{1,0:T(8,128)S(1)} fusion(bf16[1024,2048,1]{1,0,2:T(8,128)(2,1)} %bitcast.11, pred[256,2,1024]{2,1,0:T(4,128)(4,1)S(1)} %eq.76), kind=kOutput, calls=%fused_computation.18 | convolution fusion | flops 2148007936 | bytes 6815744 | tf_op jit(solution)/shard_map/sp,sd->pd/dot_general | solution.py:55
  418.6 1.2 add_convert_fusion
  (23 shorter events, 1.7 us)
Async XLA Ops:
  6.5 280.4 %all-gather.3.cloned.1.call-start = ((), (), s32[]{:S(2)}) async-start(), calls=%async_computation.3 | async-start | bytes 20971520 | tf_op jit(solution)/shard_map/all_gather | solution.py:8
  18.2 109.3 %copy-start.2 = (bf16[1,2048,1024]{2,1,0:T(8,128)(2,1)S(1)}, bf16[1,2048,1024]{2,1,0:T(8,128)(2,1)}, u32[]{:S(2)}) copy-start(bf16[1,2048,1024]{2,1,0:T(8,128)(2,1)} %param.11) | copy-start | bytes 12582916
  133.5 0.8 copy-start.1
  287.0 10.3 %copy-start.3 = (f32[1,1024]{1,0:T(1,128)S(1)}, f32[1,1024]{1,0:T(1,128)}, u32[]{:S(2)}) copy-start(f32[1,1024]{1,0:T(1,128)} %param.13) | copy-start | bytes 12292
  307.2 106.7 %all-to-all-start.2 = ((bf16[64,16,2048]{2,1,0:T(8,128)(2,1)}), bf16[64,16,2048]{2,1,0:T(8,128)(2,1)}, u32[]{:S(2)}, u32[]{:S(2)}) async-start(bf16[64,16,2048]{2,1,0:T(8,128)(2,1)} %bitcast.44), calls=%async_computation.2 | async-start | bytes 8388608 | tf_op jit(solution)/shard_map/all_to_all | solution.py:53
  413.9 4.7 %copy-start = (f32[2048]{0:T(1024)S(1)}, f32[2048]{0:T(1024)}, u32[]{:S(2)}) copy-start(f32[2048]{0:T(1024)} %param.8) | copy-start | bytes 24580
Sparse Core Ops, SparseCore 0:
  133.7 153.2 all-gather.2
